TPU v7x, 256 devices: a whole 4x4x8 slice. The times are simulated.
256 devices in a mesh: dp: 16 (over x_lo, z), tensor: 16 (over y, x_hi, core).
Axes of the slice: x: 4 (x_hi: 2, x_lo: 2; x = x_hi * 2 + x_lo), y: 4, z: 8, core: 2. Of those that a mesh axis runs over, the one named last changes fastest.
Arguments:
- query_rows: bfloat16 [32768, 8192], P('dp', 'tensor'), may hold values from -16 to 16
- key_rows: bfloat16 [32768, 1024], P('dp'), may hold values from -10 to 10
- value_rows: bfloat16 [32768, 1024], P('dp'), may hold values from -600 to 600
- segment_ids: int32 [32768], P('dp'), may hold values from 0 to 127, never falling along the last dimension, each value on 1 to 512 neighbouring positions
- norm_gain: float32 [8192], replicated, may hold values from 0.1 to 1.9
- draft_weight: bfloat16 [8192, 512], P('tensor', 'dp'), may hold values from -0.0625 to 0.0625
- targets: bfloat16 [32768, 512], P(('dp', 'tensor')), may hold values from -6 to 6
Outputs:
- grad_weight: float32 [8192, 512], P('tensor', 'dp')
Inputs may be any that keep to these rules, and one draw needn't show every extreme that they name: `segment_ids`: document ids never fall along the tokens; a document has at most 512 tokens, and one has exactly 512.
All inputs are finite; a program needn't handle non-finite values.
Results may differ from a plain program's by a relative error of at most 0.0015.
Values may be sent and summed in bfloat16 or wider, within the bound.
No kernel may reach another device: no remote copies, remote signals or barrier semaphores. Data moves between devices by JAX's collectives and lax.ppermute only.
A program may use at most 128 MiB of HBM per device.

v0:
```python
import jax
import jax.numpy as jnp
from jax import lax
from jax.sharding import PartitionSpec as P

HEADS = 64
KV_HEADS = 8
HEAD_DIM = 128


def attend_local(query_rows, key_rows, value_rows, segment_ids):
    length = query_rows.shape[0]
    local_heads = query_rows.shape[1] // HEAD_DIM
    group = HEADS // KV_HEADS
    head_count = max(1, local_heads // group)
    repeats = local_heads // head_count
    first = lax.axis_index("tensor") * local_heads // group
    keys_local = lax.dynamic_slice_in_dim(
        key_rows, first * HEAD_DIM, head_count * HEAD_DIM, 1
    ).reshape(length, head_count, HEAD_DIM)
    values_local = lax.dynamic_slice_in_dim(
        value_rows, first * HEAD_DIM, head_count * HEAD_DIM, 1
    ).reshape(length, head_count, HEAD_DIM)
    grouped = query_rows.reshape(length, head_count, repeats, HEAD_DIM)
    width = min(length, 512)
    scale = HEAD_DIM ** (-0.5)
    places = jnp.arange(length, dtype=jnp.int32)

    def one_block(number):
        offset = number * width
        query_block = lax.dynamic_slice_in_dim(grouped, offset, width, 0)
        block_segments = lax.dynamic_slice_in_dim(segment_ids, offset, width, 0)
        block_places = offset + jnp.arange(width, dtype=jnp.int32)
        allowed = (block_segments[:, None] == segment_ids[None, :]) & (
            block_places[:, None] >= places[None, :]
        )
        scores = (
            jnp.einsum(
                "qgrd,kgd->grqk", query_block, keys_local, preferred_element_type=jnp.float32
            )
            * scale
        )
        scores = jnp.where(allowed[None, None], scores, -1e30)
        shifted = jnp.exp(scores - jnp.max(scores, axis=-1, keepdims=True))
        probs = (shifted / jnp.sum(shifted, axis=-1, keepdims=True)).astype(jnp.bfloat16)
        mixed = jnp.einsum(
            "grqk,kgd->qgrd", probs, values_local, preferred_element_type=jnp.float32
        )
        return mixed.astype(jnp.bfloat16).reshape(width, local_heads * HEAD_DIM)

    outputs = lax.map(one_block, jnp.arange(length // width, dtype=jnp.int32))
    return outputs.reshape(length, local_heads * HEAD_DIM)


def loss_derivative(predicted, targets, total_tokens):
    residual = predicted - targets.astype(jnp.float32)
    return (jnp.clip(residual, -1.0, 1.0) / jnp.sqrt(jnp.float32(total_tokens))).astype(
        jnp.bfloat16
    )


def on_device(query_rows, key_rows, value_rows, segment_ids, norm_gain, draft_weight, targets):
    attended = attend_local(query_rows, key_rows, value_rows, segment_ids)
    length = query_rows.shape[0]
    total_tokens = length * lax.axis_size("dp")
    weight_slab = lax.all_gather(draft_weight, "dp", axis=1, tiled=True)
    regrouped = lax.all_to_all(attended, "tensor", split_axis=0, concat_axis=1, tiled=True)
    features = regrouped.astype(jnp.float32)
    mean_square = jnp.mean(features * features, axis=-1, keepdims=True)
    normed = (features * lax.rsqrt(mean_square + 1e-06) * norm_gain[None, :]).astype(jnp.bfloat16)
    picked = normed
    predicted = jnp.dot(
        picked,
        lax.all_gather(weight_slab, "tensor", axis=0, tiled=True),
        preferred_element_type=jnp.float32,
    )
    grad_pred = loss_derivative(predicted, targets, total_tokens)
    picked = normed
    grad_slab = lax.psum_scatter(
        lax.dot_general(
            picked, grad_pred, (((0,), (0,)), ((), ())), preferred_element_type=jnp.float32
        ),
        "tensor",
        scatter_dimension=0,
        tiled=True,
    )
    return lax.psum_scatter(grad_slab, "dp", scatter_dimension=1, tiled=True)


def solution(mesh):
    placed = (
        P("dp", "tensor"),
        P("dp", None),
        P("dp", None),
        P("dp"),
        P(),
        P("tensor", "dp"),
        P(("dp", "tensor"), None),
    )
    return jax.shard_map(
        on_device, mesh=mesh, in_specs=placed, out_specs=P("tensor", "dp"), check_vma=False
    )
```

profile of v0, /device:TPU:8, one launch (start us, length us, event | category | flops | bytes accessed | tf_op | source)
XLA Modules:
  0.0 414.3 jit_solution(10289684197386694751)
XLA Ops:
  6.5 41.8 %all_gather.6 = bf16[512,512]{0,1:T(8,128)(2,1)} all-gather(bf16[512,32]{0,1:T(8,128)(2,1)} %param.14), channel_id=1, replica_groups=mesh['dp'=16,'tensor'=16] {'dp'}, dimensions={1}, use_global_device_ids=true | all-gather | bytes 557056 | tf_op jit(solution)/shard_map/all_gather | solution.py:66
  50.9 2.5 copy.16
  53.4 73.3 %while.11 = (s32[]{:T(128)}, bf16[4,512,512]{2,1,0:T(8,128)(2,1)}, s32[4]{0:T(128)S(1)}, s32[2048]{0:T(1024)S(1)}, bf16[2048,1,4,128]{0,3,2,1:T(8,128)(2,1)}, /*...) while((s32[]{:T(128)}, bf16[4,512,512]{2,1,0:T(8,128)(2,1)}, ...), condition=%wide.region_3.4_spmd.clone, body=%wide.region_0.3_spmd.clone.sunk | while | flops 2201219584 | bytes 58780336 | solution.py:51
  56.0 4.9 %fusion.38 = (f32[4,512]{1,0:T(4,128)S(1)}, f32[512,4,2048]{2,0,1:T(8,128)S(1)}) fusion(pred[512,2048]{1,0:T(8,128)(4,1)S(1)} %fusion.37, bf16[2048,1,128]{2,0,1:T(8,128)(2,1)S(1)} %get-tuple-element.168, bf16[2048,1,4,128]{0,3,2,1:T(8,128)(2,1)} %get-tuple-element.167, s32[]{:T(128)S(6)} %select_n.40), kind=kOutput, calls=%fused_computation.5.clone.1 | convolution fusion | flops 1086322688 | bytes 18882564 | tf_op jit(solution)/shard_map/while/body/eval_jaxpr/qgrd,kgd->grqk/dot_general | solution.py:38
  60.9 4.5 %fusion.39 = f32[4,512]{1,0:T(4,128)S(1)} fusion(f32[512,4,2048]{2,0,1:T(8,128)S(1)} %get-tuple-element.139, f32[4,512]{1,0:T(4,128)S(1)} %get-tuple-element.140, pred[512,2048]{1,0:T(8,128)(4,1)S(1)} %fusion.37), kind=kLoop, calls=%fused_computation.4.clone.1 | loop fusion | flops 16775168 | bytes 17842176 | tf_op jit(solution)/shard_map/while/body/eval_jaxpr/reduce_sum | solution.py:45
  65.4 5.3 %fusion.40 = bf16[4,512,128]{1,2,0:T(8,128)(2,1)S(1)} fusion(f32[4,512]{1,0:T(4,128)S(1)} %fusion.39, f32[4,512]{1,0:T(4,128)S(1)} %get-tuple-element.140, f32[512,4,2048]{2,0,1:T(8,128)S(1)} %get-tuple-element.139, pred[512,2048]{1,0:T(8,128)(4,1)S(1)} %fusion.37, bf16[2048,1,128]{0,2,1:T(8,128)(2,1)S(1)} %get-tuple-element.169), kind=kOutput, calls=%fused_computation.10.clone.1 | convolution fusion | flops 1094975488 | bytes 18890752 | tf_op jit(solution)/shard_map/while/body/eval_jaxpr/grqk,kgd->qgrd/dot_general | solution.py:46
  74.4 4.9 %fusion.38 = (f32[4,512]{1,0:T(4,128)S(1)}, f32[512,4,2048]{2,0,1:T(8,128)S(1)}) fusion(pred[512,2048]{1,0:T(8,128)(4,1)S(1)} %fusion.37, bf16[2048,1,128]{2,0,1:T(8,128)(2,1)S(1)} %get-tuple-element.168, bf16[2048,1,4,128]{0,3,2,1:T(8,128)(2,1)} %get-tuple-element.167, s32[]{:T(128)S(6)} %select_n.40), kind=kOutput, calls=%fused_computation.5.clone.1 | convolution fusion | flops 1086322688 | bytes 18882564 | tf_op jit(solution)/shard_map/while/body/eval_jaxpr/qgrd,kgd->grqk/dot_general | solution.py:38
  79.2 4.5 %fusion.39 = f32[4,512]{1,0:T(4,128)S(1)} fusion(f32[512,4,2048]{2,0,1:T(8,128)S(1)} %get-tuple-element.139, f32[4,512]{1,0:T(4,128)S(1)} %get-tuple-element.140, pred[512,2048]{1,0:T(8,128)(4,1)S(1)} %fusion.37), kind=kLoop, calls=%fused_computation.4.clone.1 | loop fusion | flops 16775168 | bytes 17842176 | tf_op jit(solution)/shard_map/while/body/eval_jaxpr/reduce_sum | solution.py:45
  83.7 5.3 %fusion.40 = bf16[4,512,128]{1,2,0:T(8,128)(2,1)S(1)} fusion(f32[4,512]{1,0:T(4,128)S(1)} %fusion.39, f32[4,512]{1,0:T(4,128)S(1)} %get-tuple-element.140, f32[512,4,2048]{2,0,1:T(8,128)S(1)} %get-tuple-element.139, pred[512,2048]{1,0:T(8,128)(4,1)S(1)} %fusion.37, bf16[2048,1,128]{0,2,1:T(8,128)(2,1)S(1)} %get-tuple-element.169), kind=kOutput, calls=%fused_computation.10.clone.1 | convolution fusion | flops 1094975488 | bytes 18890752 | tf_op jit(solution)/shard_map/while/body/eval_jaxpr/grqk,kgd->qgrd/dot_general | solution.py:46
  92.7 4.9 %fusion.38 = (f32[4,512]{1,0:T(4,128)S(1)}, f32[512,4,2048]{2,0,1:T(8,128)S(1)}) fusion(pred[512,2048]{1,0:T(8,128)(4,1)S(1)} %fusion.37, bf16[2048,1,128]{2,0,1:T(8,128)(2,1)S(1)} %get-tuple-element.168, bf16[2048,1,4,128]{0,3,2,1:T(8,128)(2,1)} %get-tuple-element.167, s32[]{:T(128)S(6)} %select_n.40), kind=kOutput, calls=%fused_computation.5.clone.1 | convolution fusion | flops 1086322688 | bytes 18882564 | tf_op jit(solution)/shard_map/while/body/eval_jaxpr/qgrd,kgd->grqk/dot_general | solution.py:38
  97.6 4.5 %fusion.39 = f32[4,512]{1,0:T(4,128)S(1)} fusion(f32[512,4,2048]{2,0,1:T(8,128)S(1)} %get-tuple-element.139, f32[4,512]{1,0:T(4,128)S(1)} %get-tuple-element.140, pred[512,2048]{1,0:T(8,128)(4,1)S(1)} %fusion.37), kind=kLoop, calls=%fused_computation.4.clone.1 | loop fusion | flops 16775168 | bytes 17842176 | tf_op jit(solution)/shard_map/while/body/eval_jaxpr/reduce_sum | solution.py:45
  102.1 5.3 %fusion.40 = bf16[4,512,128]{1,2,0:T(8,128)(2,1)S(1)} fusion(f32[4,512]{1,0:T(4,128)S(1)} %fusion.39, f32[4,512]{1,0:T(4,128)S(1)} %get-tuple-element.140, f32[512,4,2048]{2,0,1:T(8,128)S(1)} %get-tuple-element.139, pred[512,2048]{1,0:T(8,128)(4,1)S(1)} %fusion.37, bf16[2048,1,128]{0,2,1:T(8,128)(2,1)S(1)} %get-tuple-element.169), kind=kOutput, calls=%fused_computation.10.clone.1 | convolution fusion | flops 1094975488 | bytes 18890752 | tf_op jit(solution)/shard_map/while/body/eval_jaxpr/grqk,kgd->qgrd/dot_general | solution.py:46
  111.0 4.9 %fusion.38 = (f32[4,512]{1,0:T(4,128)S(1)}, f32[512,4,2048]{2,0,1:T(8,128)S(1)}) fusion(pred[512,2048]{1,0:T(8,128)(4,1)S(1)} %fusion.37, bf16[2048,1,128]{2,0,1:T(8,128)(2,1)S(1)} %get-tuple-element.168, bf16[2048,1,4,128]{0,3,2,1:T(8,128)(2,1)} %get-tuple-element.167, s32[]{:T(128)S(6)} %select_n.40), kind=kOutput, calls=%fused_computation.5.clone.1 | convolution fusion | flops 1086322688 | bytes 18882564 | tf_op jit(solution)/shard_map/while/body/eval_jaxpr/qgrd,kgd->grqk/dot_general | solution.py:38
  115.9 4.5 %fusion.39 = f32[4,512]{1,0:T(4,128)S(1)} fusion(f32[512,4,2048]{2,0,1:T(8,128)S(1)} %get-tuple-element.139, f32[4,512]{1,0:T(4,128)S(1)} %get-tuple-element.140, pred[512,2048]{1,0:T(8,128)(4,1)S(1)} %fusion.37), kind=kLoop, calls=%fused_computation.4.clone.1 | loop fusion | flops 16775168 | bytes 17842176 | tf_op jit(solution)/shard_map/while/body/eval_jaxpr/reduce_sum | solution.py:45
  120.4 5.3 %fusion.40 = bf16[4,512,128]{1,2,0:T(8,128)(2,1)S(1)} fusion(f32[4,512]{1,0:T(4,128)S(1)} %fusion.39, f32[4,512]{1,0:T(4,128)S(1)} %get-tuple-element.140, f32[512,4,2048]{2,0,1:T(8,128)S(1)} %get-tuple-element.139, pred[512,2048]{1,0:T(8,128)(4,1)S(1)} %fusion.37, bf16[2048,1,128]{0,2,1:T(8,128)(2,1)S(1)} %get-tuple-element.169), kind=kOutput, calls=%fused_computation.10.clone.1 | convolution fusion | flops 1094975488 | bytes 18890752 | tf_op jit(solution)/shard_map/while/body/eval_jaxpr/grqk,kgd->qgrd/dot_general | solution.py:46
  126.7 33.7 %all_to_all.13 = bf16[16,128,512]{2,1,0:T(8,128)(2,1)S(1)} all-to-all(bf16[16,128,512]{2,1,0:T(8,128)(2,1)} %bitcast.86), channel_id=1, replica_groups=mesh['dp'=16,'tensor'=16] {'tensor'}, dimensions={0} | all-to-all | bytes 4194304 | tf_op jit(solution)/shard_map/all_to_all | solution.py:67
  160.5 2.5 convert_bitcast_fusion
  163.0 5.3 %copy.20 = f32[128,16,512]{0,2,1:T(8,128)} copy(f32[128,16,512]{2,0,1:T(8,128)} %convert_bitcast_fusion) | data formatting | bytes 8388608 | tf_op jit(solution)/shard_map/convert_element_type | solution.py:68
  168.9 2.9 fusion.20
  171.8 6.3 %fusion.23 = bf16[128,512]{1,0:T(8,128)(2,1)S(1)} fusion(bf16[128,8192]{0,1:T(8,128)(2,1)S(1)} %fusion.20, bf16[8192,512]{0,1:T(8,128)(2,1)} %all-gather.2.cloned.1.call-done, bf16[128,512]{1,0:T(8,128)(2,1)S(1)} %copy-done.2), kind=kOutput, calls=%fused_computation.30 | convolution fusion | flops 1074069504 | bytes 10747904 | tf_op jit(solution)/shard_map/dot_general | solution.py:72
  178.1 8.0 %fusion.24 = f32[8192,512]{1,0:T(8,128)} fusion(bf16[128,8192]{0,1:T(8,128)(2,1)S(1)} %fusion.20, bf16[128,512]{1,0:T(8,128)(2,1)S(1)} %fusion.23), kind=kOutput, calls=%fused_computation.34 | convolution fusion | flops 1073741824 | bytes 19005440 | tf_op jit(solution)/shard_map/dot_general | solution.py:80
  186.2 147.4 %reduce-scatter.5.cloned.1.call-done = f32[512,512]{1,0:T(8,128)} async-done(((f32[8192,512]{1,0:T(8,128)}), f32[512,512]{1,0:T(8,128)}) %reduce-scatter.5.cloned.1.call-update) | async-done | bytes 1048592 | tf_op jit(solution)/shard_map/reduce_scatter | solution.py:79
  333.6 2.5 copy.22
  336.1 71.6 %reduce-scatter.7.cloned.1.call-done = f32[32,512]{1,0:T(8,128)} async-done(((f32[512,512]{1,0:T(8,128)}), f32[32,512]{1,0:T(8,128)}) %reduce-scatter.7.cloned.1.call-update) | async-done | bytes 65552
  (46 shorter events, 15.0 us)
Async XLA Ops:
  6.5 44.3 %copy-start = (bf16[2048,512]{1,0:T(8,128)(2,1)S(1)}, bf16[2048,512]{1,0:T(8,128)(2,1)}, u32[]{:S(2)}) copy-start(bf16[2048,512]{1,0:T(8,128)(2,1)} %param.9) | copy-start | bytes 6291460
  6.5 46.9 %copy-start.1 = (s32[2048]{0:T(1024)S(1)}, s32[2048]{0:T(1024)}, u32[]{:S(2)}) copy-start(s32[2048]{0:T(1024)} %param.12) | copy-start | bytes 24580
  6.5 165.2 %all-gather.2.cloned.1.call-start = ((), (), s32[]{:S(2)}) async-start(), calls=%async_computation.3 | async-start | bytes 8912896 | tf_op jit(solution)/shard_map/all_gather | solution.py:74
  48.4 285.2 %reduce-scatter.5.cloned.1.call-start = ((), (), s32[]{:S(2)}) async-start(), calls=%async_computation.4 | async-start | bytes 17825792 | tf_op jit(solution)/shard_map/reduce_scatter | solution.py:79
  163.0 5.9 %copy-start.3 = (f32[8192]{0:T(1024)S(1)}, f32[8192]{0:T(1024)}, u32[]{:S(2)}) copy-start(f32[8192]{0:T(1024)} %param.13) | copy-start | bytes 98308
  168.4 3.4 copy-start.2
  186.1 221.6 %reduce-scatter.7.cloned.1.call-start = ((), (), s32[]{:S(2)}) async-start(), calls=%async_computation.5 | async-start | bytes 1114112
Sparse Core Ops, SparseCore 0:
  48.5 75.7 all-gather.1
  186.2 147.2 reduce-scatter.4
  336.3 71.4 reduce-scatter.6
where the time goes:
time: 415 us; the launch traced here: 414 us
  waiting for transfers between devices  219 us (53%)
  blocking collectives  75.5 us (18%)
  matrix products  55 us (13%)
  other arithmetic  28.6 us (7%)
  local copies, waits for them, and re-layouts  20 us (5%)
  between operations  13.2 us (3%)
    reduce_scatter x1, waiting for transfers between devices, on_device(): lax.psum_scatter(lax.dot_general(picked, grad_pred, (((0,), (0,)), ((), (...  147 us
    unnamed x4, waiting for transfers between devices  71.7 us
    all_gather x1, blocking collectives, on_device(): weight_slab = lax.all_gather(draft_weight, 'dp', axis=1, tiled=True)  41.8 us
    all_to_all x1, blocking collectives, on_device(): lax.all_to_all(attended, 'tensor', split_axis=0, concat_axis=1, tiled=True)  33.7 us
    dot_general x4, matrix products, one_block(): jnp.einsum('grqk,kgd->qgrd', probs, values_local, preferred_element_type=...  21.1 us
    dot_general x4, matrix products, one_block(): jnp.einsum('qgrd,kgd->grqk', query_block, keys_local, preferred_element_t...  19.5 us
    reduce_sum x4, other arithmetic, one_block(): jnp.sum(shifted, axis=-1, keepdims=True)  17.9 us
  transfers between devices with their start and end apart: 3, of which 2 were waited for; matrix products, arithmetic and copies ran while one was open for 21% of the time, Pallas kernels for 0%

commit v1 on v0

--- a/solution.py
+++ b/solution.py
@@ -63,7 +63,8 @@
     attended = attend_local(query_rows, key_rows, value_rows, segment_ids)
     length = query_rows.shape[0]
     total_tokens = length * lax.axis_size("dp")
-    weight_slab = lax.all_gather(draft_weight, "dp", axis=1, tiled=True)
+    stack = jnp.stack([draft_weight] * lax.axis_size("dp"))
+    weight_slab = jnp.concatenate(lax.all_to_all(stack, "dp", 0, 0), axis=1)
     regrouped = lax.all_to_all(attended, "tensor", split_axis=0, concat_axis=1, tiled=True)
     features = regrouped.astype(jnp.float32)
     mean_square = jnp.mean(features * features, axis=-1, keepdims=True)

time: 415 us -> 398 us (0.959)
  blocking collectives: 75.5 us -> 33.7 us
  waiting for transfers between devices: 219 us -> 231 us
  starting transfers between devices: 0.08 us -> 9.62 us
    all_gather x1 -> x0, blocking collectives: 41.8 us -> none  [on_device(): weight_slab = lax.all_gather(draft_weight, 'dp', axis=1, tiled=True)]
    all_to_all x0 -> x1, waiting for transfers between devices: none -> 9.89 us  [on_device(): weight_slab = jnp.concatenate(lax.all_to_all(stack, 'dp', 0, 0), axis=1)]
    all_to_all x0 -> x1, starting transfers between devices: none -> 9.5 us  [on_device(): weight_slab = jnp.concatenate(lax.all_to_all(stack, 'dp', 0, 0), axis=1)]
  transfers between devices with their start and end apart: 3 -> 4, of which waited for: 2 -> 3; matrix products, arithmetic and copies ran while one was open for 21% -> 22% of each run, Pallas kernels for 0% -> 0%
where the time goes in v1:
time: 398 us; the launch traced here: 397 us
  waiting for transfers between devices  231 us (58%)
  matrix products  55 us (14%)
  blocking collectives  33.7 us (8%)
  other arithmetic  28.5 us (7%)
  local copies, waits for them, and re-layouts  23 us (6%)
  between operations  13.2 us (3%)
  starting transfers between devices  9.62 us (2%)
    reduce_scatter x1, waiting for transfers between devices, on_device(): lax.psum_scatter(lax.dot_general(picked, grad_pred, (((0,), (0,)), ((), (...  150 us
    unnamed x4, waiting for transfers between devices  71.8 us
    all_to_all x1, blocking collectives, on_device(): lax.all_to_all(attended, 'tensor', split_axis=0, concat_axis=1, tiled=True)  33.7 us
    dot_general x4, matrix products, one_block(): jnp.einsum('grqk,kgd->qgrd', probs, values_local, preferred_element_type=...  21.1 us
    dot_general x4, matrix products, one_block(): jnp.einsum('qgrd,kgd->grqk', query_block, keys_local, preferred_element_t...  19.5 us
    reduce_sum x4, other arithmetic, one_block(): jnp.sum(shifted, axis=-1, keepdims=True)  17.9 us
    all_to_all x1, waiting for transfers between devices, on_device(): weight_slab = jnp.concatenate(lax.all_to_all(stack, 'dp', 0, 0), axis=1)  9.89 us
    all_to_all x1, starting transfers between devices, on_device(): weight_slab = jnp.concatenate(lax.all_to_all(stack, 'dp', 0, 0), axis=1)  9.5 us
  transfers between devices with their start and end apart: 4, of which 3 were waited for; matrix products, arithmetic and copies ran while one was open for 22% of the time, Pallas kernels for 0%

profile of v1, /device:TPU:8, one launch (start us, length us, event | category | flops | bytes accessed | tf_op | source)
XLA Modules:
  0.0 397.1 jit_solution(16283340770302144688)
XLA Ops:
  8.3 9.5 %all-to-all-start.1 = ((bf16[16,512,32]{1,2,0:T(8,128)(2,1)}), bf16[16,512,32]{1,2,0:T(8,128)(2,1)S(1)}, u32[]{:S(2)}, u32[]{:S(2)}) async-start(bf16[16,512,32]{1,2,0:T(8,128)(2,1)} %stack.2), calls=%async_computation.1 | async-start | bytes 1048576 | tf_op jit(solution)/shard_map/all_to_all | solution.py:67
  23.6 9.9 %all-to-all-done.1 = bf16[16,512,32]{1,2,0:T(8,128)(2,1)S(1)} async-done(((bf16[16,512,32]{1,2,0:T(8,128)(2,1)}), bf16[16,512,32]{1,2,0:T(8,128)(2,1)S(1)}, u32[]{:S(2)}, u32[]{:S(2)}) %all-to-all-start.1) | async-done | bytes 524320 | tf_op jit(solution)/shard_map/all_to_all | solution.py:67
  34.4 72.9 %while.11 = (s32[]{:T(128)}, bf16[4,512,512]{2,1,0:T(8,128)(2,1)}, s32[4]{0:T(128)S(1)}, s32[2048]{0:T(1024)S(1)}, bf16[2048,1,4,128]{0,3,2,1:T(8,128)(2,1)}, /*...) while((s32[]{:T(128)}, bf16[4,512,512]{2,1,0:T(8,128)(2,1)}, ...), condition=%wide.region_3.4_spmd.clone, body=%wide.region_0.3_spmd.clone.sunk | while | flops 2201219584 | bytes 58780336 | solution.py:51
  36.9 4.9 %fusion.38 = (f32[4,512]{1,0:T(4,128)S(1)}, f32[512,4,2048]{2,0,1:T(8,128)S(1)}) fusion(pred[512,2048]{1,0:T(8,128)(4,1)S(1)} %fusion.37, bf16[2048,1,128]{2,0,1:T(8,128)(2,1)S(1)} %get-tuple-element.168, bf16[2048,1,4,128]{0,3,2,1:T(8,128)(2,1)} %get-tuple-element.167, s32[]{:T(128)S(6)} %select_n.40), kind=kOutput, calls=%fused_computation.5.clone.1 | convolution fusion | flops 1086322688 | bytes 18882564 | tf_op jit(solution)/shard_map/while/body/eval_jaxpr/qgrd,kgd->grqk/dot_general | solution.py:38
  41.8 4.5 %fusion.39 = f32[4,512]{1,0:T(4,128)S(1)} fusion(f32[512,4,2048]{2,0,1:T(8,128)S(1)} %get-tuple-element.139, f32[4,512]{1,0:T(4,128)S(1)} %get-tuple-element.140, pred[512,2048]{1,0:T(8,128)(4,1)S(1)} %fusion.37), kind=kLoop, calls=%fused_computation.4.clone.1 | loop fusion | flops 16775168 | bytes 17842176 | tf_op jit(solution)/shard_map/while/body/eval_jaxpr/reduce_sum | solution.py:45
  46.3 5.3 %fusion.40 = bf16[4,512,128]{1,2,0:T(8,128)(2,1)S(1)} fusion(f32[4,512]{1,0:T(4,128)S(1)} %fusion.39, f32[4,512]{1,0:T(4,128)S(1)} %get-tuple-element.140, f32[512,4,2048]{2,0,1:T(8,128)S(1)} %get-tuple-element.139, pred[512,2048]{1,0:T(8,128)(4,1)S(1)} %fusion.37, bf16[2048,1,128]{0,2,1:T(8,128)(2,1)S(1)} %get-tuple-element.169), kind=kOutput, calls=%fused_computation.10.clone.1 | convolution fusion | flops 1094975488 | bytes 18890752 | tf_op jit(solution)/shard_map/while/body/eval_jaxpr/grqk,kgd->qgrd/dot_general | solution.py:46
  55.1 4.9 %fusion.38 = (f32[4,512]{1,0:T(4,128)S(1)}, f32[512,4,2048]{2,0,1:T(8,128)S(1)}) fusion(pred[512,2048]{1,0:T(8,128)(4,1)S(1)} %fusion.37, bf16[2048,1,128]{2,0,1:T(8,128)(2,1)S(1)} %get-tuple-element.168, bf16[2048,1,4,128]{0,3,2,1:T(8,128)(2,1)} %get-tuple-element.167, s32[]{:T(128)S(6)} %select_n.40), kind=kOutput, calls=%fused_computation.5.clone.1 | convolution fusion | flops 1086322688 | bytes 18882564 | tf_op jit(solution)/shard_map/while/body/eval_jaxpr/qgrd,kgd->grqk/dot_general | solution.py:38
  60.0 4.5 %fusion.39 = f32[4,512]{1,0:T(4,128)S(1)} fusion(f32[512,4,2048]{2,0,1:T(8,128)S(1)} %get-tuple-element.139, f32[4,512]{1,0:T(4,128)S(1)} %get-tuple-element.140, pred[512,2048]{1,0:T(8,128)(4,1)S(1)} %fusion.37), kind=kLoop, calls=%fused_computation.4.clone.1 | loop fusion | flops 16775168 | bytes 17842176 | tf_op jit(solution)/shard_map/while/body/eval_jaxpr/reduce_sum | solution.py:45
  64.5 5.3 %fusion.40 = bf16[4,512,128]{1,2,0:T(8,128)(2,1)S(1)} fusion(f32[4,512]{1,0:T(4,128)S(1)} %fusion.39, f32[4,512]{1,0:T(4,128)S(1)} %get-tuple-element.140, f32[512,4,2048]{2,0,1:T(8,128)S(1)} %get-tuple-element.139, pred[512,2048]{1,0:T(8,128)(4,1)S(1)} %fusion.37, bf16[2048,1,128]{0,2,1:T(8,128)(2,1)S(1)} %get-tuple-element.169), kind=kOutput, calls=%fused_computation.10.clone.1 | convolution fusion | flops 1094975488 | bytes 18890752 | tf_op jit(solution)/shard_map/while/body/eval_jaxpr/grqk,kgd->qgrd/dot_general | solution.py:46
  73.3 4.9 %fusion.38 = (f32[4,512]{1,0:T(4,128)S(1)}, f32[512,4,2048]{2,0,1:T(8,128)S(1)}) fusion(pred[512,2048]{1,0:T(8,128)(4,1)S(1)} %fusion.37, bf16[2048,1,128]{2,0,1:T(8,128)(2,1)S(1)} %get-tuple-element.168, bf16[2048,1,4,128]{0,3,2,1:T(8,128)(2,1)} %get-tuple-element.167, s32[]{:T(128)S(6)} %select_n.40), kind=kOutput, calls=%fused_computation.5.clone.1 | convolution fusion | flops 1086322688 | bytes 18882564 | tf_op jit(solution)/shard_map/while/body/eval_jaxpr/qgrd,kgd->grqk/dot_general | solution.py:38
  78.2 4.5 %fusion.39 = f32[4,512]{1,0:T(4,128)S(1)} fusion(f32[512,4,2048]{2,0,1:T(8,128)S(1)} %get-tuple-element.139, f32[4,512]{1,0:T(4,128)S(1)} %get-tuple-element.140, pred[512,2048]{1,0:T(8,128)(4,1)S(1)} %fusion.37), kind=kLoop, calls=%fused_computation.4.clone.1 | loop fusion | flops 16775168 | bytes 17842176 | tf_op jit(solution)/shard_map/while/body/eval_jaxpr/reduce_sum | solution.py:45
  82.7 5.3 %fusion.40 = bf16[4,512,128]{1,2,0:T(8,128)(2,1)S(1)} fusion(f32[4,512]{1,0:T(4,128)S(1)} %fusion.39, f32[4,512]{1,0:T(4,128)S(1)} %get-tuple-element.140, f32[512,4,2048]{2,0,1:T(8,128)S(1)} %get-tuple-element.139, pred[512,2048]{1,0:T(8,128)(4,1)S(1)} %fusion.37, bf16[2048,1,128]{0,2,1:T(8,128)(2,1)S(1)} %get-tuple-element.169), kind=kOutput, calls=%fused_computation.10.clone.1 | convolution fusion | flops 1094975488 | bytes 18890752 | tf_op jit(solution)/shard_map/while/body/eval_jaxpr/grqk,kgd->qgrd/dot_general | solution.py:46
  91.5 4.9 %fusion.38 = (f32[4,512]{1,0:T(4,128)S(1)}, f32[512,4,2048]{2,0,1:T(8,128)S(1)}) fusion(pred[512,2048]{1,0:T(8,128)(4,1)S(1)} %fusion.37, bf16[2048,1,128]{2,0,1:T(8,128)(2,1)S(1)} %get-tuple-element.168, bf16[2048,1,4,128]{0,3,2,1:T(8,128)(2,1)} %get-tuple-element.167, s32[]{:T(128)S(6)} %select_n.40), kind=kOutput, calls=%fused_computation.5.clone.1 | convolution fusion | flops 1086322688 | bytes 18882564 | tf_op jit(solution)/shard_map/while/body/eval_jaxpr/qgrd,kgd->grqk/dot_general | solution.py:38
  96.4 4.5 %fusion.39 = f32[4,512]{1,0:T(4,128)S(1)} fusion(f32[512,4,2048]{2,0,1:T(8,128)S(1)} %get-tuple-element.139, f32[4,512]{1,0:T(4,128)S(1)} %get-tuple-element.140, pred[512,2048]{1,0:T(8,128)(4,1)S(1)} %fusion.37), kind=kLoop, calls=%fused_computation.4.clone.1 | loop fusion | flops 16775168 | bytes 17842176 | tf_op jit(solution)/shard_map/while/body/eval_jaxpr/reduce_sum | solution.py:45
  100.9 5.3 %fusion.40 = bf16[4,512,128]{1,2,0:T(8,128)(2,1)S(1)} fusion(f32[4,512]{1,0:T(4,128)S(1)} %fusion.39, f32[4,512]{1,0:T(4,128)S(1)} %get-tuple-element.140, f32[512,4,2048]{2,0,1:T(8,128)S(1)} %get-tuple-element.139, pred[512,2048]{1,0:T(8,128)(4,1)S(1)} %fusion.37, bf16[2048,1,128]{0,2,1:T(8,128)(2,1)S(1)} %get-tuple-element.169), kind=kOutput, calls=%fused_computation.10.clone.1 | convolution fusion | flops 1094975488 | bytes 18890752 | tf_op jit(solution)/shard_map/while/body/eval_jaxpr/grqk,kgd->qgrd/dot_general | solution.py:46
  107.2 33.7 %all_to_all.18 = bf16[16,128,512]{2,1,0:T(8,128)(2,1)S(1)} all-to-all(bf16[16,128,512]{2,1,0:T(8,128)(2,1)} %bitcast.89), channel_id=1, replica_groups=mesh['dp'=16,'tensor'=16] {'tensor'}, dimensions={0} | all-to-all | bytes 4194304 | tf_op jit(solution)/shard_map/all_to_all | solution.py:68
  140.9 2.5 convert_bitcast_fusion
  143.4 5.3 %copy.21 = f32[128,16,512]{0,2,1:T(8,128)} copy(f32[128,16,512]{2,0,1:T(8,128)} %convert_bitcast_fusion) | data formatting | bytes 8388608 | tf_op jit(solution)/shard_map/convert_element_type | solution.py:69
  149.3 2.9 fusion.20
  152.2 6.3 %fusion.23 = bf16[128,512]{1,0:T(8,128)(2,1)S(1)} fusion(bf16[128,8192]{0,1:T(8,128)(2,1)S(1)} %fusion.20, bf16[8192,512]{0,1:T(8,128)(2,1)} %all-gather.2.cloned.1.call-done, bf16[128,512]{1,0:T(8,128)(2,1)S(1)} %copy-done.4), kind=kOutput, calls=%fused_computation.30 | convolution fusion | flops 1074069504 | bytes 10747904 | tf_op jit(solution)/shard_map/dot_general | solution.py:73
  158.5 8.0 %fusion.24 = f32[8192,512]{1,0:T(8,128)} fusion(bf16[128,8192]{0,1:T(8,128)(2,1)S(1)} %fusion.20, bf16[128,512]{1,0:T(8,128)(2,1)S(1)} %fusion.23), kind=kOutput, calls=%fused_computation.34 | convolution fusion | flops 1073741824 | bytes 19005440 | tf_op jit(solution)/shard_map/dot_general | solution.py:81
  166.6 149.7 %reduce-scatter.5.cloned.1.call-done = f32[512,512]{1,0:T(8,128)} async-done(((f32[8192,512]{1,0:T(8,128)}), f32[512,512]{1,0:T(8,128)}) %reduce-scatter.5.cloned.1.call-update) | async-done | bytes 1048592 | tf_op jit(solution)/shard_map/reduce_scatter | solution.py:80
  316.3 2.5 copy.23
  318.9 71.7 %reduce-scatter.7.cloned.1.call-done = f32[32,512]{1,0:T(8,128)} async-done(((f32[512,512]{1,0:T(8,128)}), f32[32,512]{1,0:T(8,128)}) %reduce-scatter.7.cloned.1.call-update) | async-done | bytes 65552
  (52 shorter events, 20.6 us)
Async XLA Ops:
  6.5 13.5 %copy-start = (bf16[2048,512]{1,0:T(8,128)(2,1)S(1)}, bf16[2048,512]{1,0:T(8,128)(2,1)}, u32[]{:S(2)}) copy-start(bf16[2048,512]{1,0:T(8,128)(2,1)} %param.9) | copy-start | bytes 6291460
  8.3 25.2 %all-to-all-start.1 = ((bf16[16,512,32]{1,2,0:T(8,128)(2,1)}), bf16[16,512,32]{1,2,0:T(8,128)(2,1)S(1)}, u32[]{:S(2)}, u32[]{:S(2)}) async-start(bf16[16,512,32]{1,2,0:T(8,128)(2,1)} %stack.2), calls=%async_computation.1 | async-start | bytes 1048576 | tf_op jit(solution)/shard_map/all_to_all | solution.py:67
  17.8 16.5 %copy-start.3 = (s32[2048]{0:T(1024)S(1)}, s32[2048]{0:T(1024)}, u32[]{:S(2)}) copy-start(s32[2048]{0:T(1024)} %param.12) | copy-start | bytes 24580
  17.8 134.3 %all-gather.2.cloned.1.call-start = ((), (), s32[]{:S(2)}) async-start(), calls=%async_computation.4 | async-start | bytes 8912896 | tf_op jit(solution)/shard_map/all_gather | solution.py:75
  20.0 14.3 %copy-start.2 = (bf16[2048,128]{0,1:T(8,128)(2,1)S(1)}, bf16[2048,128]{0,1:T(8,128)(2,1)}, u32[]{:S(2)}) copy-start(bf16[2048,128]{0,1:T(8,128)(2,1)} %copy.18) | copy-start | bytes 1572868
  33.5 0.8 copy-start.1
  34.3 282.0 %reduce-scatter.5.cloned.1.call-start = ((), (), s32[]{:S(2)}) async-start(), calls=%async_computation.5 | async-start | bytes 17825792 | tf_op jit(solution)/shard_map/reduce_scatter | solution.py:80
  143.4 5.8 %copy-start.5 = (f32[8192]{0:T(1024)S(1)}, f32[8192]{0:T(1024)}, u32[]{:S(2)}) copy-start(f32[8192]{0:T(1024)} %param.13) | copy-start | bytes 98308
  148.8 3.4 copy-start.4
  166.5 224.1 %reduce-scatter.7.cloned.1.call-start = ((), (), s32[]{:S(2)}) async-start(), calls=%async_computation.6 | async-start | bytes 1114112
Sparse Core Ops, SparseCore 0:
  34.4 78.0 all-gather.1
  166.7 149.6 reduce-scatter.4
  319.0 71.5 reduce-scatter.6
